TPU v7x, 256 devices: a whole 4x4x8 slice. The times are simulated.
256 devices in a mesh: rows: 64 (over x, z, core), cols: 4 (over y).
Axes of the slice: x: 4, y: 4, z: 8, core: 2. Of those that a mesh axis runs over, the one named last changes fastest.
Arguments:
- slot_tile: int32 [64, 3], replicated, may hold values from 0 to 128, as said below
- slot_ranks: int32 [64, 3, 4], P('rows', None, 'cols'), may hold values from 0 to 256, as said below
- diag_ranks: int32 [4], P('cols'), may hold values from 32 to 256
- panel_left_factors: bfloat16 [4, 192, 1024, 256], P('cols', 'rows'), may hold values from -12 to 12
- panel_v: bfloat16 [4, 192, 1024, 256], P('cols', 'rows'), may hold values from -0.1875 to 0.1875
- diag_u: bfloat16 [4, 1024, 256], P('cols'), may hold values from -0.38 to 0.38, as said below
- diag_v: bfloat16 [4, 1024, 256], P('cols'), may hold values from -1 to 1
- panel_points: int32 [192, 2, 1024], P('rows', None, 'cols'), may hold values from 0 to 1023, as said below
- diag_points: int32 [2, 1024], replicated, may hold values from 0 to 1023, as said below
- rhs_diag: float32 [1024, 512], P(None, 'cols'), may hold values from -0.3 to 0.3
- rhs_rest: float32 [128, 4, 4, 64, 512], P(None, 'cols', None, 'rows'), may hold values from -6 to 6
Outputs:
- panel_factor: bfloat16 [192, 1024, 1024], P('rows', 'cols')
- diag_solution: float32 [1024, 512], P(None, 'cols')
- rhs_out: float32 [128, 4, 4, 64, 512], P(None, 'cols', None, 'rows')
Inputs may be any that keep to these rules, and one draw needn't show every extreme that they name: `slot_tile`: every tile 0 to 127 stands in exactly one slot; 128 marks an empty slot; the live slots of an owner come first; every owner has 1 to 3 live slots and some owner has 3. Owners are chosen by the tiles' summed ranks. `slot_ranks`: live slots have ranks 32 to 256, empty slots 0; both 32 and 256 occur. The columns of each diag_u[j] are orthogonal, with lengths 0.1 to 0.38. `panel_points`: row 0 holds x, row 1 holds y. A live slot holds the cells of a block of 32 x (32) grid cells in some order; blocks of different tiles and of the diagonal tile are distinct; an empty slot holds the points of some tile. `diag_points`: row 0 holds x, row 1 holds y: the cells of one block of 32 x (32) grid cells in some order.
All inputs are finite; a program needn't handle non-finite values.
Results may differ from a plain program's by a relative error of at most 0.0057.
Values may be sent and summed in bfloat16 or wider, within the bound.
A program may use at most 128 MiB of HBM per device.

v0:
```python
import jax
import jax.numpy as jnp
from jax import lax
from jax.sharding import PartitionSpec as P

GX = 1024
length_scale = 0.3
nugget = 1.0


def matern(first_x, first_y, second_x, second_y):
    spacing = 1.0 / GX
    delta_x = (first_x - second_x) * spacing
    delta_y = (first_y - second_y) * spacing
    scaled = jnp.sqrt(3.0) * jnp.sqrt(delta_x * delta_x + delta_y * delta_y) / length_scale
    return (1.0 + scaled) * jnp.exp(-scaled)


def owner_rows(slot_tile, tile_count, per_peer, row_devices):
    flat_tiles = slot_tile.reshape(-1)
    slot_count = flat_tiles.shape[0]
    tmax_local = slot_tile.shape[1]
    owner_slot = (
        jnp.zeros((tile_count + 1,), jnp.int32)
        .at[flat_tiles]
        .set(jnp.arange(slot_count, dtype=jnp.int32))[:tile_count]
    )
    source_row = owner_slot // tmax_local
    source_place = owner_slot % tmax_local
    step_index = jnp.arange(per_peer, dtype=jnp.int32)
    return (
        (source_place[:, None] * per_peer + step_index[None, :]) * row_devices + source_row[:, None]
    ).reshape(-1)


def times_block(owned_rows, forward):
    return jnp.dot(
        owned_rows,
        lax.all_gather(forward, "cols", axis=1, tiled=True),
        preferred_element_type=jnp.float32,
    )


def per_device(
    slot_tile,
    slot_ranks,
    diag_ranks,
    panel_left_factors,
    panel_v,
    diag_u,
    diag_v,
    panel_points,
    diag_points,
    rhs_diag,
    rhs_rest,
):
    row_devices = lax.axis_size("rows")
    col_devices = lax.axis_size("cols")
    slot_count = panel_left_factors.shape[1]
    tile_order = diag_u.shape[1]
    rank_max = diag_u.shape[2]
    quarter = tile_order // col_devices
    per_peer = quarter // row_devices
    tile_count = rhs_rest.shape[0]
    row_index = lax.axis_index("rows")
    rank_index = jnp.arange(rank_max, dtype=jnp.int32)
    diag_mask = (rank_index < diag_ranks[0]).astype(jnp.bfloat16)
    diagonal_left_factor = diag_u[0] * diag_mask[None, :]
    diagonal_right_factor = diag_v[0] * diag_mask[None, :]
    slot_mask = (rank_index[None, :] < slot_ranks[0, :, 0][:, None]).astype(jnp.bfloat16)
    slot_left_factor = panel_left_factors[0] * slot_mask[:, None, :]
    slot_right_factor = panel_v[0] * slot_mask[:, None, :]
    inner_product_core = jnp.einsum(
        "gok,oe->gke", slot_right_factor, diagonal_right_factor, preferred_element_type=jnp.float32
    ).astype(jnp.bfloat16)
    low_rows = jnp.einsum(
        "lgc,lcz->lgz", slot_left_factor, inner_product_core, preferred_element_type=jnp.float32
    ).astype(jnp.bfloat16)
    diag_core = jnp.einsum(
        "br,bq->rq",
        diagonal_right_factor,
        diagonal_right_factor,
        preferred_element_type=jnp.float32,
    ).astype(jnp.bfloat16)
    diag_low = jnp.dot(diagonal_left_factor, diag_core, preferred_element_type=jnp.float32).astype(
        jnp.bfloat16
    )
    gathered_low, gathered_left = (
        lax.all_gather(diag_low[None], "cols", axis=0, tiled=True),
        lax.all_gather(diagonal_left_factor[None], "cols", axis=0, tiled=True),
    )
    outgoing_low = low_rows.reshape(slot_count, col_devices, quarter, rank_max)
    update_term = jnp.einsum(
        "sjnr,jbr->snb",
        lax.all_to_all(outgoing_low, "cols", split_axis=1, concat_axis=1, tiled=True),
        gathered_left,
        preferred_element_type=jnp.float32,
    )
    centre = diag_points.astype(jnp.float32)
    identity = jnp.eye(tile_order, dtype=jnp.float32)
    diag_term = jnp.einsum(
        "jbr,jcr->bc", gathered_low, gathered_left, preferred_element_type=jnp.float32
    )
    own_block = matern(centre[0][:, None], centre[1][:, None], centre[0], centre[1])
    diag_system = own_block + nugget * identity - diag_term
    factor = jnp.linalg.cholesky(diag_system)
    inverse = jax.scipy.linalg.solve_triangular(factor, identity, lower=True)
    my_tiles = lax.dynamic_slice_in_dim(slot_tile, row_index, 1, 0)[0]
    live_mask = (my_tiles < tile_count).astype(jnp.float32)
    coords = panel_points.astype(jnp.float32)
    generated = matern(coords[:, 0, :, None], coords[:, 1, :, None], centre[0], centre[1])
    system_rows = live_mask[:, None, None] * (generated - update_term)
    panel_factor = jnp.einsum(
        "snb,cb->snc", system_rows, inverse, precision=lax.Precision.HIGHEST
    ).astype(jnp.bfloat16)
    diag_solution = jnp.dot(inverse, rhs_diag, precision=lax.Precision.HIGHEST)
    forward = diag_solution.astype(jnp.bfloat16)
    pick_rows = owner_rows(slot_tile, tile_count, per_peer, row_devices)
    outgoing_rows = panel_factor.reshape(slot_count, per_peer, row_devices, tile_order)
    incoming = lax.all_to_all(outgoing_rows, "rows", split_axis=2, concat_axis=2, tiled=True)
    owned_rows = jnp.take(incoming.reshape(-1, tile_order), pick_rows, axis=0)
    product = times_block(owned_rows, forward).astype(jnp.bfloat16)
    rhs_out = rhs_rest - product.reshape(rhs_rest.shape).astype(jnp.float32)
    return (panel_factor, diag_solution, rhs_out)


def solution(mesh):
    return jax.shard_map(
        per_device,
        mesh=mesh,
        in_specs=(
            P(),
            P("rows", None, "cols"),
            P("cols"),
            P("cols", "rows", None, None),
            P("cols", "rows", None, None),
            P("cols", None, None),
            P("cols", None, None),
            P("rows", None, "cols"),
            P(),
            P(None, "cols"),
            P(None, "cols", None, "rows", None),
        ),
        out_specs=(P("rows", "cols", None), P(None, "cols"), P(None, "cols", None, "rows", None)),
        check_vma=False,
    )
```

profile of v0, /device:TPU:1, one launch (start us, length us, event | category | flops | bytes accessed | tf_op | source)
XLA Modules:
  0.0 559.6 jit_solution(14840995524542032224)
XLA Ops:
  13.1 3.7 convolution_convert_fusion
  18.1 5.0 all-to-all-start
  27.1 34.0 %all-gather.5.cloned.1.call-done = bf16[4,1024,256]{2,1,0:T(8,128)(2,1)} async-done(((bf16[1,1024,256]{2,1,0:T(8,128)(2,1)}), bf16[4,1024,256]{2,1,0:T(8,128)(2,1)}) %all-gather.5.cloned.1.call-update) | async-done | bytes 2097168 | tf_op jit(solution)/shard_map/all_gather | solution.py:90
  61.1 36.7 %all-gather.9.cloned.1.call-done = bf16[4096,256]{1,0:T(8,128)(2,1)} async-done(((bf16[1024,256]{1,0:T(8,128)(2,1)}), bf16[4096,256]{1,0:T(8,128)(2,1)}) %all-gather.9.cloned.1.call-update) | async-done | bytes 2097168 | tf_op jit(solution)/shard_map/all_gather | solution.py:89
  97.8 6.6 %convolution_bitcast_fusion = f32[1024,1024]{1,0:T(8,128)} fusion(bf16[4,1024,256]{2,1,0:T(8,128)(2,1)} %bitcast.174, bf16[4,1024,256]{2,1,0:T(8,128)(2,1)} %all-gather.5.cloned.1.call-done), kind=kOutput, calls=%fused_computation.28 | convolution fusion | flops 2147483648 | bytes 8388608 | tf_op jit(solution)/shard_map/jbr,jcr->bc/dot_general | solution.py:101
  104.4 5.3 copy.22
  109.7 9.6 %fusion.3 = f32[1024,1024]{1,0:T(8,128)S(1)} fusion(f32[1024,1024]{0,1:T(8,128)} %copy.22, f32[1024,1024]{1,0:T(8,128)} %convolution_bitcast_fusion, f32[1024]{0:T(1024)S(1)} %bitcast.169, f32[1024]{0:T(1024)S(1)} %bitcast.167), kind=kLoop, calls=%fused_computation.9 | loop fusion | flops 33554432 | bytes 12591104 | tf_op jit(solution)/shard_map/jit(cholesky)/div | solution.py:106
  121.3 11.7 %cholesky.224 = f32[128,128]{1,0:T(8,128)S(1)} custom-call(f32[128,128]{1,0:T(8,128)S(1)} %cholesky.583), custom_call_target="Cholesky" | custom-call | tf_op jit(solution)/shard_map/jit(cholesky)/cholesky | solution.py:106
  133.0 9.8 %custom-call.63 = f32[1,128,128]{1,2,0:T(8,128)S(1)} custom-call(f32[1,128,128]{2,1,0:T(8,128)S(1)} %get-tuple-element.67), custom_call_target="InvertDiagBlocksLowerTriangular" | custom-call | tf_op jit(solution)/shard_map/jit(cholesky)/cholesky | solution.py:106
  149.3 11.7 %cholesky.245 = f32[128,128]{1,0:T(8,128)S(1)} custom-call(f32[128,128]{1,0:T(8,128)S(1)} %cholesky.587), custom_call_target="Cholesky" | custom-call | tf_op jit(solution)/shard_map/jit(cholesky)/cholesky | solution.py:106
  161.6 10.2 %custom-call.64 = f32[1,128,128]{1,2,0:T(8,128)S(1)} custom-call(f32[1,128,128]{2,1,0:T(8,128)S(1)} %get-tuple-element.64), custom_call_target="InvertDiagBlocksLowerTriangular" | custom-call | tf_op jit(solution)/shard_map/jit(cholesky)/cholesky | solution.py:106
  175.2 11.7 %cholesky.470 = f32[128,128]{1,0:T(8,128)S(1)} custom-call(f32[128,128]{1,0:T(8,128)S(1)} %cholesky.592), custom_call_target="Cholesky" | custom-call | tf_op jit(solution)/shard_map/jit(cholesky)/cholesky | solution.py:106
  188.3 9.8 %custom-call.65 = f32[1,128,128]{1,2,0:T(8,128)S(1)} custom-call(f32[1,128,128]{2,1,0:T(8,128)S(1)} %get-tuple-element.61), custom_call_target="InvertDiagBlocksLowerTriangular" | custom-call | tf_op jit(solution)/shard_map/jit(cholesky)/cholesky | solution.py:106
  201.6 11.9 %cholesky.489 = f32[128,128]{1,0:T(8,128)S(1)} custom-call(f32[128,128]{1,0:T(8,128)S(1)} %cholesky.597), custom_call_target="Cholesky" | custom-call | tf_op jit(solution)/shard_map/jit(cholesky)/cholesky | solution.py:106
  214.8 9.8 %custom-call.66 = f32[1,128,128]{1,2,0:T(8,128)S(1)} custom-call(f32[1,128,128]{2,1,0:T(8,128)S(1)} %get-tuple-element.58), custom_call_target="InvertDiagBlocksLowerTriangular" | custom-call | tf_op jit(solution)/shard_map/jit(cholesky)/cholesky | solution.py:106
  228.1 11.7 %cholesky.508 = f32[128,128]{1,0:T(8,128)S(1)} custom-call(f32[128,128]{1,0:T(8,128)S(1)} %cholesky.602), custom_call_target="Cholesky" | custom-call | tf_op jit(solution)/shard_map/jit(cholesky)/cholesky | solution.py:106
  241.1 9.8 %custom-call.67 = f32[1,128,128]{1,2,0:T(8,128)S(1)} custom-call(f32[1,128,128]{2,1,0:T(8,128)S(1)} %get-tuple-element.55), custom_call_target="InvertDiagBlocksLowerTriangular" | custom-call | tf_op jit(solution)/shard_map/jit(cholesky)/cholesky | solution.py:106
  254.4 11.7 %cholesky.528 = f32[128,128]{1,0:T(8,128)S(1)} custom-call(f32[128,128]{1,0:T(8,128)S(1)} %cholesky.607), custom_call_target="Cholesky" | custom-call | tf_op jit(solution)/shard_map/jit(cholesky)/cholesky | solution.py:106
  267.5 9.8 %custom-call.68 = f32[1,128,128]{1,2,0:T(8,128)S(1)} custom-call(f32[1,128,128]{2,1,0:T(8,128)S(1)} %get-tuple-element.52), custom_call_target="InvertDiagBlocksLowerTriangular" | custom-call | tf_op jit(solution)/shard_map/jit(cholesky)/cholesky | solution.py:106
  280.3 11.7 %cholesky.548 = f32[128,128]{1,0:T(8,128)S(1)} custom-call(f32[128,128]{1,0:T(8,128)S(1)} %cholesky.612), custom_call_target="Cholesky" | custom-call | tf_op jit(solution)/shard_map/jit(cholesky)/cholesky | solution.py:106
  293.3 10.2 %custom-call.69 = f32[1,128,128]{1,2,0:T(8,128)S(1)} custom-call(f32[1,128,128]{2,1,0:T(8,128)S(1)} %get-tuple-element.49), custom_call_target="InvertDiagBlocksLowerTriangular" | custom-call | tf_op jit(solution)/shard_map/jit(cholesky)/cholesky | solution.py:106
  306.2 11.7 %cholesky.566 = f32[128,128]{1,0:T(8,128)S(1)} custom-call(f32[128,128]{1,0:T(8,128)S(1)} %convolution_subtract_fusion.11), custom_call_target="Cholesky" | custom-call | tf_op jit(solution)/shard_map/jit(cholesky)/cholesky | solution.py:106
  324.9 4.8 select_select_fusion
  329.7 27.4 %while.1 = (s32[]{:T(128)}, f32[1024,1024]{1,0:T(8,128)}, s32[8,2]{0,1:T(2,128)S(1)}, f32[8,128,128]{2,1,0:T(8,128)}, s32[]{:T(128)}) while((s32[]{:T(128)}, f32[1024,1024]{1,0:T(8,128)}, s32[8,2]{0,1:T(2,128)S(1)}, f32[8,128,128]{2,1,0:T(8,128)}, s32[]{:T(128)}) %tuple.66), condition=%wide.while_cond, body=%wide.while_body.sunk | while | flops 2 | bytes 132705 | solution.py:107
  357.1 79.6 %custom-call.70 = f32[8,128,128]{1,2,0:T(8,128)S(1)} custom-call(f32[8,128,128]{2,1,0:T(8,128)} %get-tuple-element.10), custom_call_target="InvertDiagBlocksLowerTriangular" | custom-call | tf_op jit(solution)/shard_map/jit(_solve_triangular)/triangular_solve | solution.py:107
  461.2 3.5 convolution_subtract_fusion.3
  466.2 3.4 fusion.27
  469.6 16.3 %fusion.29 = bf16[3,256,1024]{2,1,0:T(8,128)(2,1)S(1)} fusion(f32[1024,1024]{1,0:T(8,128)} %convolution_dynamic-update-slice_fusion, f32[3,256,1024,1]{2,1,0,3:T(8,128)S(1)} %fusion.27, f32[1024]{0:T(1024)S(1)} %bitcast.170, f32[3,256]{1,0:T(4,128)S(1)} %get-tuple-element.84, f32[1024]{0:T(1024)S(1)} %bitcast.168, f32[3,256]{1,0:T(4,128)S(1)} %get-tuple-element.85, ...), kind=kOutput, calls=%fused_computation.40 | convolution fusion | flops 9674686464 | bytes 8927244 | tf_op jit(solution)/shard_map/snb,cb->snc/dot_general | solution.py:113
  489.4 11.0 %all-to-all-start.1 = ((bf16[3,4,64,1024]{3,1,0,2:T(4,128)(2,1)}), bf16[3,4,64,1024]{3,1,0,2:T(4,128)(2,1)}, u32[]{:S(2)}, u32[]{:S(2)}) async-start(bf16[3,4,64,1024]{3,1,0,2:T(4,128)(2,1)} %copy.24), calls=%async_computation.1 | async-start | bytes 3145728 | tf_op jit(solution)/shard_map/all_to_all | solution.py:120
  500.7 6.5 %fusion.142 = (bf16[1024,128]{1,0:T(8,128)(2,1)}, f32[1024,128]{1,0:T(8,128)}) fusion(f32[1024,1024]{1,0:T(8,128)} %convolution_dynamic-update-slice_fusion, f32[1024,128]{1,0:T(8,128)S(1)} %copy-done), kind=kOutput, calls=%fused_computation.240 | convolution fusion | flops 1610743808 | bytes 5505024 | tf_op jit(solution)/shard_map/dot_general | solution.py:116
  509.0 31.1 %all-to-all-done.1 = bf16[3,4,64,1024]{3,1,0,2:T(4,128)(2,1)} async-done(((bf16[3,4,64,1024]{3,1,0,2:T(4,128)(2,1)}), bf16[3,4,64,1024]{3,1,0,2:T(4,128)(2,1)}, u32[]{:S(2)}, u32[]{:S(2)}) %all-to-all-start.1) | async-done | bytes 1572896 | tf_op jit(solution)/shard_map/all_to_all | solution.py:120
  544.7 3.4 fusion.52
  (136 shorter events, 115.5 us)
Async XLA Ops:
  7.2 493.5 %copy-start = (f32[1024,128]{1,0:T(8,128)S(1)}, f32[1024,128]{1,0:T(8,128)}, u32[]{:S(2)}) copy-start(f32[1024,128]{1,0:T(8,128)} %param.20) | copy-start | bytes 1572868
  7.2 5.9 %copy-start.9 = (bf16[1,1024,256]{2,1,0:T(8,128)(2,1)S(1)}, bf16[1,1024,256]{2,1,0:T(8,128)(2,1)}, u32[]{:S(2)}) copy-start(bf16[1,1024,256]{2,1,0:T(8,128)(2,1)} %param.17) | copy-start | bytes 1572868
  7.2 5.8 %copy-start.8 = (s32[1,3,1]{1,2,0:T(1,128)S(1)}, s32[1,3,1]{1,2,0:T(1,128)}, u32[]{:S(2)}) copy-start(s32[1,3,1]{1,2,0:T(1,128)} %param.12) | copy-start | bytes 40
  7.2 53.9 %all-gather.5.cloned.1.call-start = ((), (), s32[]{:S(2)}) async-start(), calls=%async_computation.2 | async-start | bytes 2621440 | tf_op jit(solution)/shard_map/all_gather | solution.py:90
  9.9 87.9 %all-gather.9.cloned.1.call-start = ((), (), s32[]{:S(2)}) async-start(), calls=%async_computation.4 | async-start | bytes 2621440 | tf_op jit(solution)/shard_map/all_gather | solution.py:89
  16.8 6.3 %copy-start.6 = (s32[2,1024]{1,0:T(2,128)S(1)}, s32[2,1024]{1,0:T(2,128)}, u32[]{:S(2)}) copy-start(s32[2,1024]{1,0:T(2,128)} %param.19) | copy-start | bytes 24580
  16.8 6.3 %copy-start.7 = (s32[3,2,256]{2,1,0:T(2,128)S(1)}, s32[3,2,256]{2,1,0:T(2,128)}, u32[]{:S(2)}) copy-start(s32[3,2,256]{2,1,0:T(2,128)} %param.18) | copy-start | bytes 18436
  16.8 6.3 %copy-start.5 = (s32[64,3]{0,1:T(4,128)S(1)}, s32[64,3]{0,1:T(4,128)}, u32[]{:S(2)}) copy-start(s32[64,3]{0,1:T(4,128)} %param.11) | copy-start | bytes 2308
  18.1 448.1 %all-to-all-start = ((bf16[3,4,256,256]{3,2,0,1:T(8,128)(2,1)}), bf16[3,4,256,256]{3,2,0,1:T(8,128)(2,1)S(1)}, u32[]{:S(2)}, u32[]{:S(2)}) async-start(bf16[3,4,256,256]{3,2,0,1:T(8,128)(2,1)} %copy.20), calls=%async_computation | async-start | bytes 3145728 | tf_op jit(solution)/shard_map/all_to_all | solution.py:95
  119.3 2.0 copy-start.2
  436.7 5.6 %copy-start.1 = (f32[1024,1024]{1,0:T(8,128)S(1)}, f32[1024,1024]{1,0:T(8,128)}, u32[]{:S(2)}) copy-start(f32[1024,1024]{1,0:T(8,128)} %fusion.42) | copy-start | bytes 12582916
  485.9 1.1 copy-start.3
  489.4 50.7 %all-to-all-start.1 = ((bf16[3,4,64,1024]{3,1,0,2:T(4,128)(2,1)}), bf16[3,4,64,1024]{3,1,0,2:T(4,128)(2,1)}, u32[]{:S(2)}, u32[]{:S(2)}) async-start(bf16[3,4,64,1024]{3,1,0,2:T(4,128)(2,1)} %copy.24), calls=%async_computation.1 | async-start | bytes 3145728 | tf_op jit(solution)/shard_map/all_to_all | solution.py:120
  500.4 44.4 %all-gather.7.cloned.1.call-start = ((), (), s32[]{:S(2)}) async-start(), calls=%async_computation.3 | async-start | bytes 1310720 | tf_op jit(solution)/shard_map/all_gather | solution.py:39
  544.7 5.9 %copy-start.4 = (f32[128,1,4,1,512]{4,3,2,1,0:T(1,128)S(1)}, f32[128,1,4,1,512]{4,3,2,1,0:T(1,128)}, u32[]{:S(2)}) copy-start(f32[128,1,4,1,512]{4,3,2,1,0:T(1,128)} %param.21) | copy-start | bytes 3145732
Sparse Core Ops, SparseCore 0:
  10.0 51.0 all-gather.4
  63.5 34.2 all-gather.8
  507.3 26.3 all-gather.6
where the time goes:
time: 567 us; the launch traced here: 560 us
  other arithmetic  275 us (49%)
  waiting for transfers between devices  102 us (18%)
  matrix products  95.5 us (17%)
  local copies, waits for them, and re-layouts  50.8 us (9%)
  between operations  20.4 us (4%)
  starting transfers between devices  16.4 us (3%)
    another operation x30, other arithmetic, per_device(): factor = jnp.linalg.cholesky(diag_system)  172 us
    another operation x3, other arithmetic, per_device(): inverse = jax.scipy.linalg.solve_triangular(factor, identity, lower=True)  84.4 us
    all_gather x1, waiting for transfers between devices, per_device(): lax.all_gather(diag_low[None], 'cols', axis=0, tiled=True)  36.7 us
    all_gather x1, waiting for transfers between devices, per_device(): lax.all_gather(diagonal_left_factor[None], 'cols', axis=0, tiled=True)  34 us
    all_to_all x1, waiting for transfers between devices, per_device(): lax.all_to_all(outgoing_rows, 'rows', split_axis=2, concat_axis=2, tiled=...  31.1 us
    another operation x15, matrix products, per_device(): inverse = jax.scipy.linalg.solve_triangular(factor, identity, lower=True)  29.4 us
    another operation x24, local copies, waits for them, and re-layouts  27.4 us
    another operation x14, matrix products, per_device(): factor = jnp.linalg.cholesky(diag_system)  23.3 us
  transfers between devices with their start and end apart: 5, of which 3 were waited for; matrix products, arithmetic and copies ran while one was open for 69% of the time, Pallas kernels for 0%

commit v1 on v0

--- a/solution.py
+++ b/solution.py
@@ -6,6 +6,27 @@
 GX = 1024
 length_scale = 0.3
 nugget = 1.0
+
+
+def ring_gather(x, axis, dim):
+    length, index, rows = (lax.axis_size(axis), lax.axis_index(axis), x.shape[dim])
+    upward = [(i, (i + 1) % length) for i in range(length)]
+    left = [(i, (i - 1) % length) for i in range(length)]
+    out = jnp.zeros((*x.shape[:dim], length * rows, *x.shape[dim + 1 :]), x.dtype)
+    out = lax.dynamic_update_slice_in_dim(out, x, index * rows, axis=dim)
+    from_left = from_right = x
+    halfway = length // 2
+    for step in range(1, halfway + 1):
+        from_left = lax.ppermute(from_left, axis, upward)
+        out = lax.dynamic_update_slice_in_dim(
+            out, from_left, (index - step) % length * rows, axis=dim
+        )
+        if step < length - halfway:
+            from_right = lax.ppermute(from_right, axis, left)
+            out = lax.dynamic_update_slice_in_dim(
+                out, from_right, (index + step) % length * rows, axis=dim
+            )
+    return out
 
 
 def matern(first_x, first_y, second_x, second_y):
@@ -86,7 +107,7 @@
         jnp.bfloat16
     )
     gathered_low, gathered_left = (
-        lax.all_gather(diag_low[None], "cols", axis=0, tiled=True),
+        ring_gather(diag_low[None], "cols", 0),
         lax.all_gather(diagonal_left_factor[None], "cols", axis=0, tiled=True),
     )
     outgoing_low = low_rows.reshape(slot_count, col_devices, quarter, rank_max)

time: 567 us -> 547 us (0.965)
  waiting for transfers between devices: 102 us -> 69.9 us
    ppermute x0 -> x3, waiting for transfers between devices: none -> 38.8 us  [the longest x2 38.8 us: ring_gather(): from_left = lax.ppermute(from_left, axis, upward)]
    all_gather x1 -> x0, waiting for transfers between devices: 36.7 us -> none  [per_device(): lax.all_gather(diag_low[None], 'cols', axis=0, tiled=True)]
    all_gather x1, waiting for transfers between devices: 34 us -> 0.02 us  [per_device(): lax.all_gather(diagonal_left_factor[None], 'cols', axis=0, tiled=True)]
  transfers between devices with their start and end apart: 5 -> 7, of which waited for: 3 -> 2; matrix products, arithmetic and copies ran while one was open for 69% -> 73% of each run, Pallas kernels for 0% -> 0%
where the time goes in v1:
time: 547 us; the launch traced here: 538 us
  other arithmetic  275 us (50%)
  matrix products  96 us (18%)
  waiting for transfers between devices  69.9 us (13%)
  local copies, waits for them, and re-layouts  54.7 us (10%)
  starting transfers between devices  22 us (4%)
  between operations  20.7 us (4%)
    another operation x30, other arithmetic, per_device(): factor = jnp.linalg.cholesky(diag_system)  173 us
    another operation x3, other arithmetic, per_device(): inverse = jax.scipy.linalg.solve_triangular(factor, identity, lower=True)  84.4 us
    ppermute x2, waiting for transfers between devices, ring_gather(): from_left = lax.ppermute(from_left, axis, upward)  38.8 us
    all_to_all x1, waiting for transfers between devices, per_device(): lax.all_to_all(outgoing_rows, 'rows', split_axis=2, concat_axis=2, tiled=...  31.1 us
    another operation x15, matrix products, per_device(): inverse = jax.scipy.linalg.solve_triangular(factor, identity, lower=True)  29.4 us
    another operation x24, local copies, waits for them, and re-layouts  27.5 us
    another operation x14, matrix products, per_device(): factor = jnp.linalg.cholesky(diag_system)  23.3 us
    dot_general x1, matrix products, per_device(): jnp.einsum('snb,cb->snc', system_rows, inverse, precision=lax.Precision.H...  16.3 us
  transfers between devices with their start and end apart: 7, of which 2 were waited for; matrix products, arithmetic and copies ran while one was open for 73% of the time, Pallas kernels for 0%

profile of v1, /device:TPU:1, one launch (start us, length us, event | category | flops | bytes accessed | tf_op | source)
XLA Modules:
  0.0 537.9 jit_solution(17912168035515724245)
XLA Ops:
  10.0 3.1 constant_dynamic-update-slice_fusion.29
  16.7 5.0 convolution_convert_fusion
  24.3 4.5 all-to-all-start
  35.4 38.8 %collective-permute-done.2 = bf16[1,1024,256]{2,1,0:T(8,128)(2,1)} collective-permute-done((bf16[1,1024,256]{2,1,0:T(8,128)(2,1)S(1)}, bf16[1,1024,256]{2,1,0:T(8,128)(2,1)}, u32[]{:S(2)}, u32[]{:S(2)}) %collective-permute-start.2) | collective-permute-done | bytes 524320 | tf_op jit(solution)/shard_map/ppermute | solution.py:20
  75.3 5.9 %convolution_bitcast_fusion = f32[1024,1024]{1,0:T(8,128)} fusion(bf16[4,1024,256]{2,1,0:T(8,128)(2,1)S(1)} %constant_dynamic-update-slice_fusion.26, bf16[4,1024,256]{2,1,0:T(8,128)(2,1)} %all-gather.3.cloned.1.call-done), kind=kOutput, calls=%fused_computation.28 | convolution fusion | flops 2147483648 | bytes 8388608 | tf_op jit(solution)/shard_map/jbr,jcr->bc/dot_general | solution.py:122
  81.2 5.3 copy.22
  86.5 9.6 %fusion.3 = f32[1024,1024]{1,0:T(8,128)S(1)} fusion(f32[1024,1024]{0,1:T(8,128)} %copy.22, f32[1024,1024]{1,0:T(8,128)} %convolution_bitcast_fusion, f32[1024]{0:T(1024)S(1)} %bitcast.174, f32[1024]{0:T(1024)S(1)} %bitcast.172), kind=kLoop, calls=%fused_computation.9 | loop fusion | flops 33554432 | bytes 12591104 | tf_op jit(solution)/shard_map/jit(cholesky)/div | solution.py:127
  98.1 11.7 %cholesky.224 = f32[128,128]{1,0:T(8,128)S(1)} custom-call(f32[128,128]{1,0:T(8,128)S(1)} %cholesky.583), custom_call_target="Cholesky" | custom-call | tf_op jit(solution)/shard_map/jit(cholesky)/cholesky | solution.py:127
  112.4 9.8 %custom-call.63 = f32[1,128,128]{1,2,0:T(8,128)S(1)} custom-call(f32[1,128,128]{2,1,0:T(8,128)S(1)} %get-tuple-element.67), custom_call_target="InvertDiagBlocksLowerTriangular" | custom-call | tf_op jit(solution)/shard_map/jit(cholesky)/cholesky | solution.py:127
  126.1 11.7 %cholesky.245 = f32[128,128]{1,0:T(8,128)S(1)} custom-call(f32[128,128]{1,0:T(8,128)S(1)} %cholesky.587), custom_call_target="Cholesky" | custom-call | tf_op jit(solution)/shard_map/jit(cholesky)/cholesky | solution.py:127
  138.5 10.2 %custom-call.64 = f32[1,128,128]{1,2,0:T(8,128)S(1)} custom-call(f32[1,128,128]{2,1,0:T(8,128)S(1)} %get-tuple-element.64), custom_call_target="InvertDiagBlocksLowerTriangular" | custom-call | tf_op jit(solution)/shard_map/jit(cholesky)/cholesky | solution.py:127
  152.0 11.7 %cholesky.470 = f32[128,128]{1,0:T(8,128)S(1)} custom-call(f32[128,128]{1,0:T(8,128)S(1)} %cholesky.592), custom_call_target="Cholesky" | custom-call | tf_op jit(solution)/shard_map/jit(cholesky)/cholesky | solution.py:127
  165.1 9.8 %custom-call.65 = f32[1,128,128]{1,2,0:T(8,128)S(1)} custom-call(f32[1,128,128]{2,1,0:T(8,128)S(1)} %get-tuple-element.61), custom_call_target="InvertDiagBlocksLowerTriangular" | custom-call | tf_op jit(solution)/shard_map/jit(cholesky)/cholesky | solution.py:127
  178.4 11.9 %cholesky.489 = f32[128,128]{1,0:T(8,128)S(1)} custom-call(f32[128,128]{1,0:T(8,128)S(1)} %cholesky.597), custom_call_target="Cholesky" | custom-call | tf_op jit(solution)/shard_map/jit(cholesky)/cholesky | solution.py:127
  191.6 9.8 %custom-call.66 = f32[1,128,128]{1,2,0:T(8,128)S(1)} custom-call(f32[1,128,128]{2,1,0:T(8,128)S(1)} %get-tuple-element.58), custom_call_target="InvertDiagBlocksLowerTriangular" | custom-call | tf_op jit(solution)/shard_map/jit(cholesky)/cholesky | solution.py:127
  204.9 11.7 %cholesky.508 = f32[128,128]{1,0:T(8,128)S(1)} custom-call(f32[128,128]{1,0:T(8,128)S(1)} %cholesky.602), custom_call_target="Cholesky" | custom-call | tf_op jit(solution)/shard_map/jit(cholesky)/cholesky | solution.py:127
  218.0 9.8 %custom-call.67 = f32[1,128,128]{1,2,0:T(8,128)S(1)} custom-call(f32[1,128,128]{2,1,0:T(8,128)S(1)} %get-tuple-element.55), custom_call_target="InvertDiagBlocksLowerTriangular" | custom-call | tf_op jit(solution)/shard_map/jit(cholesky)/cholesky | solution.py:127
  231.3 11.7 %cholesky.528 = f32[128,128]{1,0:T(8,128)S(1)} custom-call(f32[128,128]{1,0:T(8,128)S(1)} %cholesky.607), custom_call_target="Cholesky" | custom-call | tf_op jit(solution)/shard_map/jit(cholesky)/cholesky | solution.py:127
  244.4 9.8 %custom-call.68 = f32[1,128,128]{1,2,0:T(8,128)S(1)} custom-call(f32[1,128,128]{2,1,0:T(8,128)S(1)} %get-tuple-element.52), custom_call_target="InvertDiagBlocksLowerTriangular" | custom-call | tf_op jit(solution)/shard_map/jit(cholesky)/cholesky | solution.py:127
  257.2 11.7 %cholesky.548 = f32[128,128]{1,0:T(8,128)S(1)} custom-call(f32[128,128]{1,0:T(8,128)S(1)} %cholesky.612), custom_call_target="Cholesky" | custom-call | tf_op jit(solution)/shard_map/jit(cholesky)/cholesky | solution.py:127
  270.2 10.2 %custom-call.69 = f32[1,128,128]{1,2,0:T(8,128)S(1)} custom-call(f32[1,128,128]{2,1,0:T(8,128)S(1)} %get-tuple-element.49), custom_call_target="InvertDiagBlocksLowerTriangular" | custom-call | tf_op jit(solution)/shard_map/jit(cholesky)/cholesky | solution.py:127
  283.0 11.7 %cholesky.566 = f32[128,128]{1,0:T(8,128)S(1)} custom-call(f32[128,128]{1,0:T(8,128)S(1)} %slice_subtract_fusion.6), custom_call_target="Cholesky" | custom-call | tf_op jit(solution)/shard_map/jit(cholesky)/cholesky | solution.py:127
  301.7 4.8 select_select_fusion
  306.6 27.5 %while.1 = (s32[]{:T(128)}, f32[1024,1024]{1,0:T(8,128)}, s32[8,2]{0,1:T(2,128)S(1)}, f32[8,128,128]{2,1,0:T(8,128)}, s32[]{:T(128)}) while((s32[]{:T(128)}, f32[1024,1024]{1,0:T(8,128)}, s32[8,2]{0,1:T(2,128)S(1)}, f32[8,128,128]{2,1,0:T(8,128)}, s32[]{:T(128)}) %tuple.67), condition=%wide.while_cond, body=%wide.while_body.sunk | while | flops 2 | bytes 132705 | solution.py:128
  334.1 79.6 %custom-call.70 = f32[8,128,128]{1,2,0:T(8,128)S(1)} custom-call(f32[8,128,128]{2,1,0:T(8,128)} %get-tuple-element.10), custom_call_target="InvertDiagBlocksLowerTriangular" | custom-call | tf_op jit(solution)/shard_map/jit(_solve_triangular)/triangular_solve | solution.py:128
  438.2 3.5 convolution_subtract_fusion.3
  443.1 3.2 fusion.27
  446.3 16.3 %fusion.29 = bf16[3,256,1024]{2,1,0:T(8,128)(2,1)S(1)} fusion(f32[1024,1024]{1,0:T(8,128)} %convolution_dynamic-update-slice_fusion, f32[3,256,1024,1]{2,1,0,3:T(8,128)S(1)} %fusion.27, f32[1024]{0:T(1024)S(1)} %bitcast.175, f32[3,256]{1,0:T(4,128)S(1)} %get-tuple-element.86, f32[1024]{0:T(1024)S(1)} %bitcast.173, f32[3,256]{1,0:T(4,128)S(1)} %get-tuple-element.87, ...), kind=kOutput, calls=%fused_computation.40 | convolution fusion | flops 9674686464 | bytes 8927244 | tf_op jit(solution)/shard_map/snb,cb->snc/dot_general | solution.py:134
  466.1 12.2 %all-to-all-start.1 = ((bf16[3,4,64,1024]{3,1,0,2:T(4,128)(2,1)}), bf16[3,4,64,1024]{3,1,0,2:T(4,128)(2,1)}, u32[]{:S(2)}, u32[]{:S(2)}) async-start(bf16[3,4,64,1024]{3,1,0,2:T(4,128)(2,1)} %copy.24), calls=%async_computation.1 | async-start | bytes 3145728 | tf_op jit(solution)/shard_map/all_to_all | solution.py:141
  478.7 6.5 %fusion.162 = (bf16[1024,128]{1,0:T(8,128)(2,1)}, f32[1024,128]{1,0:T(8,128)}) fusion(f32[1024,1024]{1,0:T(8,128)} %convolution_dynamic-update-slice_fusion, f32[1024,128]{1,0:T(8,128)S(1)} %copy-done), kind=kOutput, calls=%fused_computation.252 | convolution fusion | flops 1610743808 | bytes 5505024 | tf_op jit(solution)/shard_map/dot_general | solution.py:137
  487.0 31.1 %all-to-all-done.1 = bf16[3,4,64,1024]{3,1,0,2:T(4,128)(2,1)} async-done(((bf16[3,4,64,1024]{3,1,0,2:T(4,128)(2,1)}), bf16[3,4,64,1024]{3,1,0,2:T(4,128)(2,1)}, u32[]{:S(2)}, u32[]{:S(2)}) %all-to-all-start.1) | async-done | bytes 1572896 | tf_op jit(solution)/shard_map/all_to_all | solution.py:141
  522.7 3.4 fusion.52
  (143 shorter events, 121.3 us)
Async XLA Ops:
  7.2 471.5 %copy-start = (f32[1024,128]{1,0:T(8,128)S(1)}, f32[1024,128]{1,0:T(8,128)}, u32[]{:S(2)}) copy-start(f32[1024,128]{1,0:T(8,128)} %param.20) | copy-start | bytes 1572868
  7.2 9.4 %copy-start.8 = (s32[1,3,1]{1,2,0:T(1,128)S(1)}, s32[1,3,1]{1,2,0:T(1,128)}, u32[]{:S(2)}) copy-start(s32[1,3,1]{1,2,0:T(1,128)} %param.12) | copy-start | bytes 40
  7.2 68.1 %all-gather.3.cloned.1.call-start = ((), (), s32[]{:S(2)}) async-start(), calls=%async_computation.2 | async-start | bytes 2621440 | tf_op jit(solution)/shard_map/all_gather | solution.py:111
  13.0 19.6 %collective-permute-start = (bf16[1,1024,256]{2,1,0:T(8,128)(2,1)}, bf16[1,1024,256]{2,1,0:T(8,128)(2,1)S(1)}, u32[]{:S(2)}, u32[]{:S(2)}) collective-permute-start(bf16[1,1024,256]{2,1,0:T(8,128)(2,1)} %get-tuple-element.75), channel_id=1, source_target_pairs={{0,1},{1,2},{2,3},{3,0},{4,5},{5,6},{6,7},{7,4},{8,9},{9,10},{10,1... | collective-permute-start | bytes 1572872 | tf_op jit(solution)/shard_map/ppermute | solution.py:20
  15.2 19.1 %collective-permute-start.1 = (bf16[1,1024,256]{2,1,0:T(8,128)(2,1)}, bf16[1,1024,256]{2,1,0:T(8,128)(2,1)}, u32[]{:S(2)}, u32[]{:S(2)}) collective-permute-start(bf16[1,1024,256]{2,1,0:T(8,128)(2,1)} %get-tuple-element.75), channel_id=1, source_target_pairs={{0,3},{1,0},{2,1},{3,2},{4,7},{5,4},{6,5},{7,6},{8,11},{9,8},{10,9... | collective-permute-start | bytes 1572872 | tf_op jit(solution)/shard_map/ppermute | solution.py:25
  21.7 7.2 %copy-start.7 = (s32[3,2,256]{2,1,0:T(2,128)S(1)}, s32[3,2,256]{2,1,0:T(2,128)}, u32[]{:S(2)}) copy-start(s32[3,2,256]{2,1,0:T(2,128)} %param.18) | copy-start | bytes 18436
  24.3 7.0 %copy-start.6 = (s32[2,1024]{1,0:T(2,128)S(1)}, s32[2,1024]{1,0:T(2,128)}, u32[]{:S(2)}) copy-start(s32[2,1024]{1,0:T(2,128)} %param.19) | copy-start | bytes 24580
  24.3 9.7 %copy-start.5 = (s32[64,3]{0,1:T(4,128)S(1)}, s32[64,3]{0,1:T(4,128)}, u32[]{:S(2)}) copy-start(s32[64,3]{0,1:T(4,128)} %param.11) | copy-start | bytes 2308
  24.3 418.7 %all-to-all-start = ((bf16[3,4,256,256]{3,2,0,1:T(8,128)(2,1)}), bf16[3,4,256,256]{3,2,0,1:T(8,128)(2,1)}, u32[]{:S(2)}, u32[]{:S(2)}) async-start(bf16[3,4,256,256]{3,2,0,1:T(8,128)(2,1)} %copy.20), calls=%async_computation | async-start | bytes 3145728 | tf_op jit(solution)/shard_map/all_to_all | solution.py:116
  32.6 41.5 %collective-permute-start.2 = (bf16[1,1024,256]{2,1,0:T(8,128)(2,1)S(1)}, bf16[1,1024,256]{2,1,0:T(8,128)(2,1)}, u32[]{:S(2)}, u32[]{:S(2)}) collective-permute-start(bf16[1,1024,256]{2,1,0:T(8,128)(2,1)S(1)} %collective-permute-done), channel_id=1, source_target_pairs={{0,1},{1,2},{2,3},{3,0},{4,5},{5,6},{6,7},{7,4},{8,9},{9,10},{10,1... | collective-permute-start | bytes 1572872 | tf_op jit(solution)/shard_map/ppermute | solution.py:20
  96.1 2.0 copy-start.2
  413.6 5.6 %copy-start.1 = (f32[1024,1024]{1,0:T(8,128)S(1)}, f32[1024,1024]{1,0:T(8,128)}, u32[]{:S(2)}) copy-start(f32[1024,1024]{1,0:T(8,128)} %fusion.42) | copy-start | bytes 12582916
  436.7 6.4 %copy-start.9 = (bf16[4,1024,256]{2,1,0:T(8,128)(2,1)S(1)}, bf16[4,1024,256]{2,1,0:T(8,128)(2,1)}, u32[]{:S(2)}) copy-start(bf16[4,1024,256]{2,1,0:T(8,128)(2,1)} %all-gather.3.cloned.1.call-done) | copy-start | bytes 6291460
  462.6 1.1 copy-start.3
  466.1 51.9 %all-to-all-start.1 = ((bf16[3,4,64,1024]{3,1,0,2:T(4,128)(2,1)}), bf16[3,4,64,1024]{3,1,0,2:T(4,128)(2,1)}, u32[]{:S(2)}, u32[]{:S(2)}) async-start(bf16[3,4,64,1024]{3,1,0,2:T(4,128)(2,1)} %copy.24), calls=%async_computation.1 | async-start | bytes 3145728 | tf_op jit(solution)/shard_map/all_to_all | solution.py:141
  478.3 44.4 %all-gather.5.cloned.1.call-start = ((), (), s32[]{:S(2)}) async-start(), calls=%async_computation.3 | async-start | bytes 1310720 | tf_op jit(solution)/shard_map/all_gather | solution.py:60
  522.7 5.9 %copy-start.4 = (f32[128,1,4,1,512]{4,3,2,1,0:T(1,128)S(1)}, f32[128,1,4,1,512]{4,3,2,1,0:T(1,128)}, u32[]{:S(2)}) copy-start(f32[128,1,4,1,512]{4,3,2,1,0:T(1,128)} %param.21) | copy-start | bytes 3145732
Sparse Core Ops, SparseCore 0:
  10.0 57.9 all-gather.2
  485.3 26.5 all-gather.4
